TPU v7x, 256 devices: a whole 4x4x8 slice. The times are simulated.
256 devices in a mesh: seq: 32 (over z_hi, x, core), fsdp: 8 (over z_lo, y).
Axes of the slice: x: 4, y: 4, z: 8 (z_hi: 4, z_lo: 2; z = z_hi * 2 + z_lo), core: 2. Of those that a mesh axis runs over, the one named last changes fastest.
Arguments:
- inputs: bfloat16 [8, 128, 32, 4096], P('fsdp', None, 'seq'), may hold values from -6 to 6
- queries: bfloat16 [8, 128, 32, 4096], P('fsdp', None, 'seq'), may hold values from -1000 to 1000
- rotated_keys: bfloat16 [8, 128, 32, 512], P('fsdp', None, 'seq'), may hold values from -6 to 6
- out_grad: bfloat16 [8, 128, 32, 4096], P('fsdp', None, 'seq'), may hold values from -6 to 6
- value_weight: bfloat16 [4096, 512], P(('seq', 'fsdp')), may hold values from -0.09375 to 0.09375
- fisher: float32 [4096, 512], P(('seq', 'fsdp')), may hold values from 0.2 to 20
- anchor: float32 [4096, 512], P(('seq', 'fsdp')), may hold values from -0.25 to 0.25
- doc_starts: int32 [8, 64], P('fsdp'), may hold values from 0 to 4064, as said below
- owners: int32 [8, 64], P('fsdp'), may hold values from 0 to 31, as said below
Outputs:
- query_grad: bfloat16 [8, 32, 6, 32, 4096], P('fsdp', 'seq')
- key_grad: bfloat16 [8, 128, 32, 512], P('fsdp', None, 'seq')
- input_grad: bfloat16 [8, 128, 32, 4096], P('fsdp', None, 'seq')
- ewc_grad: float32 [4096, 512], P(('seq', 'fsdp'))
Inputs may be any that keep to these rules, and one draw needn't show every extreme that they name: `doc_starts`: in each sequence the starts rise strictly from 0; every document's length (4096 minus the last start for the last one) is a multiple of 32. Each of the 32 owners is named by exactly two documents of a sequence; one owner's documents hold at most 192 positions in all, and in every sequence some owner holds exactly that many.
All inputs are finite; a program needn't handle non-finite values.
Results may differ from a plain program's by a relative error of at most 0.029.
Values may be sent and summed in bfloat16 or wider, within the bound.
No kernel may reach another device: no remote copies, remote signals or barrier semaphores. Data moves between devices by JAX's collectives and lax.ppermute only.
A program may use at most 128 MiB of HBM per device.

v0:
```python
import math
import jax
import jax.numpy as jnp
from jax import lax
from jax.sharding import PartitionSpec as P

KVH = 4
HD = 128
SCORE_NEG = -1e30
EWC_LAMBDA = 4.0


def round_plan(starts, owner_list, lane_count, rounds):
    round_ids = jnp.arange(rounds, dtype=jnp.int32)
    start_rounds = starts // lane_count
    doc_of = jnp.sum((start_rounds[None, :] <= round_ids[:, None]).astype(jnp.int32), axis=1) - 1
    doc_ids = jnp.arange(starts.shape[0], dtype=jnp.int32)
    onehot = (doc_of[:, None] == doc_ids[None, :]).astype(jnp.int32)
    owner_of = jnp.sum(onehot * owner_list[None, :], axis=1)
    earlier = (owner_of[:, None] == owner_of[None, :]) & (round_ids[None, :] < round_ids[:, None])
    rank_of = jnp.sum(earlier.astype(jnp.int32), axis=1)
    return (doc_of, owner_of, rank_of)


def slot_rounds(owner_of, rank_of, lane_count, capacity):
    lane_ids = jnp.arange(lane_count, dtype=jnp.int32)
    slot_ids = jnp.arange(capacity, dtype=jnp.int32)
    round_ids = jnp.arange(owner_of.shape[0], dtype=jnp.int32)
    match = (owner_of[None, None, :] == lane_ids[None, :, None]) & (
        rank_of[None, None, :] == slot_ids[:, None, None]
    )
    source = jnp.sum(match.astype(jnp.int32) * round_ids[None, None, :], axis=2)
    filled = jnp.any(match, axis=2)
    return (source, filled)


def attend(query_in, grad_in, key_in, value_in, visible):
    slot_count = query_in.shape[0] * query_in.shape[1]
    group = query_in.shape[3] // HD
    scale = 1.0 / math.sqrt(HD)
    query_parts = []
    key_parts = []
    value_parts = []
    for item_index in range(query_in.shape[2]):
        q_item = query_in[:, :, item_index, :].reshape(slot_count, group, HD)
        g_item = grad_in[:, :, item_index, :].reshape(slot_count, group, HD)
        k_item = key_in[:, :, item_index, :].reshape(slot_count, HD)
        v_item = value_in[:, :, item_index, :].reshape(slot_count, HD)
        scores = (
            jnp.einsum("mgd,kd->gmk", q_item, k_item, preferred_element_type=jnp.float32) * scale
        )
        masked = jnp.where(visible[None], scores, SCORE_NEG)
        peak = jnp.max(masked, axis=2, keepdims=True)
        probs = jnp.where(visible[None], jnp.exp(masked - peak), 0.0)
        totals = jnp.sum(probs, axis=2, keepdims=True)
        probs = probs / jnp.where(totals > 0.0, totals, 1.0)
        probs_b = probs.astype(jnp.bfloat16)
        attn_out = jnp.einsum(
            "gmk,kd->mgd", probs_b, v_item, preferred_element_type=jnp.float32
        ).astype(jnp.bfloat16)
        delta = jnp.einsum("mgd,mgd->gm", g_item, attn_out, preferred_element_type=jnp.float32)
        dprobs = jnp.einsum("mgd,kd->gmk", g_item, v_item, preferred_element_type=jnp.float32)
        dscores = (probs * (dprobs - delta[:, :, None]) * scale).astype(jnp.bfloat16)
        query_grad = jnp.einsum(
            "gmk,kd->mgd", dscores, k_item, preferred_element_type=jnp.float32
        ).astype(jnp.bfloat16)
        key_grad = jnp.einsum(
            "gmk,mgd->kd", dscores, q_item, preferred_element_type=jnp.float32
        ).astype(jnp.bfloat16)
        value_grad = jnp.einsum(
            "gmk,mgd->kd", probs_b, g_item, preferred_element_type=jnp.float32
        ).astype(jnp.bfloat16)
        query_parts.append(query_grad.reshape(query_in.shape[0], query_in.shape[1], group * HD))
        key_parts.append(key_grad.reshape(query_in.shape[0], query_in.shape[1], HD))
        value_parts.append(value_grad.reshape(query_in.shape[0], query_in.shape[1], HD))
    return (
        jnp.stack(query_parts, axis=2),
        jnp.stack(key_parts, axis=2),
        jnp.stack(value_parts, axis=2),
    )


def fetch_weight(value_weight):
    return lax.all_gather(value_weight, ("seq", "fsdp"), axis=0, tiled=True)


def body(inputs, queries, rotated_keys, out_grad, value_weight, fisher, anchor, doc_starts, owners):
    lane_count = lax.axis_size("seq")
    own_lane = lax.axis_index("seq")
    rounds = inputs.shape[1]
    capacity = 3 * rounds // (2 * lane_count)
    token_rows = inputs.reshape(rounds, inputs.shape[3])
    query_rows = queries.reshape(rounds, queries.shape[3])
    key_rows = rotated_keys.reshape(rounds, rotated_keys.shape[3])
    grad_rows = out_grad.reshape(rounds, out_grad.shape[3])
    doc_of, owner_of, rank_of = round_plan(doc_starts[0], owners[0], lane_count, rounds)
    source, filled = slot_rounds(owner_of, rank_of, lane_count, capacity)

    def to_slots(rows):
        picked = jnp.take(rows, source.reshape(-1), axis=0).reshape(capacity, lane_count, KVH, -1)
        return jnp.where(filled[:, :, None, None], picked, jnp.zeros_like(picked))

    query_send = to_slots(query_rows)
    grad_send = to_slots(grad_rows)
    key_send = to_slots(key_rows)
    my_rounds = lax.dynamic_index_in_dim(source, own_lane, 1, keepdims=False)
    my_filled = lax.dynamic_index_in_dim(filled, own_lane, 1, keepdims=False)
    lane_ids = jnp.arange(lane_count, dtype=jnp.int32)
    slot_pos = (my_rounds[:, None] * lane_count + lane_ids[None, :]).reshape(-1)
    round_doc = jnp.where(my_filled, jnp.take(doc_of, my_rounds), -1)
    slot_doc = jnp.broadcast_to(round_doc[:, None], (capacity, lane_count)).reshape(-1)
    slot_live = jnp.broadcast_to(my_filled[:, None], (capacity, lane_count)).reshape(-1)
    visible = (slot_doc[:, None] == slot_doc[None, :]) & (slot_pos[None, :] <= slot_pos[:, None])
    visible = visible & slot_live[:, None] & slot_live[None, :]
    full_weight = fetch_weight(value_weight)
    value_rows = jnp.dot(token_rows, full_weight, preferred_element_type=jnp.float32).astype(
        jnp.bfloat16
    )
    value_send = to_slots(value_rows)
    query_back, key_back, value_back = attend(
        lax.all_to_all(query_send, "seq", split_axis=1, concat_axis=1, tiled=True),
        lax.all_to_all(grad_send, "seq", split_axis=1, concat_axis=1, tiled=True),
        lax.all_to_all(key_send, "seq", split_axis=1, concat_axis=1, tiled=True),
        lax.all_to_all(value_send, "seq", split_axis=1, concat_axis=1, tiled=True),
        visible,
    )
    returned = (
        lax.all_to_all(key_back, "seq", split_axis=1, concat_axis=1, tiled=True),
        lax.all_to_all(value_back, "seq", split_axis=1, concat_axis=1, tiled=True),
    )
    flat_index = rank_of * lane_count + owner_of
    key_home = jnp.take(returned[0].reshape(capacity * lane_count, -1), flat_index, axis=0)
    value_home = jnp.take(returned[1].reshape(capacity * lane_count, -1), flat_index, axis=0)
    input_grad = jnp.einsum(
        "rk,dk->rd", value_home, full_weight, preferred_element_type=jnp.float32
    ).astype(jnp.bfloat16)
    partial_sum = jnp.einsum(
        "rd,rk->dk", token_rows, value_home, preferred_element_type=jnp.float32
    )
    summed = lax.psum_scatter(partial_sum, ("seq", "fsdp"), scatter_dimension=0, tiled=True)
    tokens_total = rounds * lane_count * lax.axis_size("fsdp")
    grad_scale = 1.0 / math.sqrt(tokens_total)
    ewc_grad = summed * grad_scale + EWC_LAMBDA * fisher * (
        value_weight.astype(jnp.float32) - anchor
    )
    query_out = query_back.reshape(1, 1, capacity, lane_count, -1)
    return (
        query_out,
        key_home.reshape(1, rounds, 1, -1),
        input_grad.reshape(1, rounds, 1, -1),
        ewc_grad,
    )


def solution(mesh):
    return jax.shard_map(
        body,
        mesh=mesh,
        in_specs=(
            P("fsdp", None, "seq", None),
            P("fsdp", None, "seq", None),
            P("fsdp", None, "seq", None),
            P("fsdp", None, "seq", None),
            P(("seq", "fsdp"), None),
            P(("seq", "fsdp"), None),
            P(("seq", "fsdp"), None),
            P("fsdp", None),
            P("fsdp", None),
        ),
        out_specs=(
            P("fsdp", "seq", None, None, None),
            P("fsdp", None, "seq", None),
            P("fsdp", None, "seq", None),
            P(("seq", "fsdp"), None),
        ),
        check_vma=False,
    )
```

profile of v0, /device:TPU:0, one launch (start us, length us, event | category | flops | bytes accessed | tf_op | source)
XLA Modules:
  0.0 2140.9 jit_solution(14226648482565059061)
XLA Ops:
  10.8 5.6 gather_fusion.4
  16.4 2.7 gather_fusion.2
  19.1 3.9 broadcast_select_fusion
  23.0 2.9 reshape.287
  25.9 3.9 reshape.283
  29.8 3.6 copy_select_fusion
  33.4 50.5 %all_to_all.30 = bf16[6,32,4,1024]{3,2,0,1:T(4,128)(2,1)} all-to-all(bf16[6,32,4,1024]{3,2,0,1:T(4,128)(2,1)S(1)} %get-tuple-element.56), channel_id=1, replica_groups=mesh['seq'=32,'fsdp'=8] {'seq'}, dimensions={1} | all-to-all | bytes 3145728 | tf_op jit(solution)/shard_map/all_to_all | solution.py:121
  83.9 5.5 all-to-all-start.3
  91.2 1.0 gather_fusion.1
  92.2 0.8 and_and_fusion
  93.0 6.2 fusion.106
  99.4 0.8 copy.470
  100.5 0.8 copy.476
  101.5 0.8 copy.474
  102.6 0.8 copy.472
  103.4 640.9 %all-gather.2.cloned.1.call-done = bf16[4096,512]{1,0:T(8,128)(2,1)} async-done(((bf16[16,512]{1,0:T(8,128)(2,1)}), bf16[4096,512]{1,0:T(8,128)(2,1)}) %all-gather.2.cloned.1.call-update) | async-done | bytes 4194320 | tf_op jit(solution)/shard_map/all_gather | solution.py:84
  744.3 2.9 convolution_convert_fusion.9
  747.2 1.0 gather_fusion.3
  748.5 1.0 copy_select_fusion.2
  749.5 34.9 %all-to-all-start = ((bf16[6,32,4,128]{3,2,0,1:T(4,128)(2,1)}), bf16[6,32,4,128]{3,2,0,1:T(4,128)(2,1)S(1)}, u32[]{:S(2)}, u32[]{:S(2)}) async-start(bf16[6,32,4,128]{3,2,0,1:T(4,128)(2,1)} %get-tuple-element.58), calls=%async_computation | async-start | bytes 393216 | tf_op jit(solution)/shard_map/all_to_all | solution.py:123
  784.4 2.3 fusion.105
  787.3 0.8 copy.477
  788.4 0.9 copy.475
  789.5 0.8 copy.473
  790.3 6.1 all-to-all-done
  796.8 1.8 fusion.115
  798.8 1.2 copy-done.10
  800.5 1.8 fusion.112
  803.0 0.9 copy-done.8
  804.4 1.8 fusion.109
  806.4 1.2 copy-done.6
  808.0 1.8 fusion.118
  810.0 1.0 copy-done.4
  811.6 1.1 pad_maximum_fusion.2
  812.7 3.9 all-to-all-start.5
  816.7 11.8 all-to-all-done.5
  828.6 0.8 gather_fusion.6
  829.5 4.6 convolution_bitcast_fusion
  834.1 9.1 copy.468
  843.2 1.0 copy-done.30
  844.3 4.0 all-to-all-start.2
  848.5 1.0 bitcast_convert_fusion.3
  849.5 10.8 all-to-all-done.2
  861.4 0.8 fusion.29
  862.7 0.9 copy-done.32
  864.1 1.0 copy.397
  865.2 1.9 stack_reshape.37
  867.1 1.7 fusion.42
  869.0 0.8 fusion.34
  870.2 0.9 copy-done.33
  872.1 1.7 fusion.43
  873.9 0.8 fusion.39
  874.7 1.2 fusion.11
  877.3 1.6 fusion.44
  879.1 0.8 fusion.24
  881.3 1.1 pad_maximum_fusion.1
  882.5 4.2 all-to-all-start.4
  887.8 1.2 copy.416
  889.1 2.4 reshape.288
  891.4 7.5 all-to-all-done.4
  899.0 1.0 gather_fusion.5
  900.8 4.7 fusion.4
  905.4 1227.0 %reduce-scatter.4.cloned.1.call-done = f32[16,512]{1,0:T(8,128)} async-done(((f32[4096,512]{1,0:T(8,128)}), f32[16,512]{1,0:T(8,128)}) %reduce-scatter.4.cloned.1.call-update) | async-done | bytes 32784 | tf_op jit(solution)/shard_map/reduce_scatter | solution.py:140
  2132.4 1.4 multiply_add_fusion
  (215 shorter events, 19.5 us)
Async XLA Ops:
  7.2 737.2 %copy-start = (bf16[1,128,1,4096]{3,1,2,0:T(8,128)(2,1)S(1)}, bf16[1,128,1,4096]{3,1,2,0:T(8,128)(2,1)}, u32[]{:S(2)}) copy-start(bf16[1,128,1,4096]{3,1,2,0:T(8,128)(2,1)} %param.15) | copy-start | bytes 3145732
  7.2 737.1 %all-gather.2.cloned.1.call-start = ((), (), s32[]{:S(2)}) async-start(), calls=%async_computation.7 | async-start | bytes 4210688 | tf_op jit(solution)/shard_map/all_gather | solution.py:84
  10.7 5.7 copy-start.2
  83.9 7.3 copy-start.3
  83.9 665.6 %all-to-all-start.3 = ((bf16[6,32,4,1024]{3,2,0,1:T(4,128)(2,1)}), bf16[6,32,4,1024]{3,2,0,1:T(4,128)(2,1)S(1)}, u32[]{:S(2)}, u32[]{:S(2)}) async-start(bf16[6,32,4,1024]{3,2,0,1:T(4,128)(2,1)} %get-tuple-element.55), calls=%async_computation.3 | async-start | bytes 3145728 | tf_op jit(solution)/shard_map/all_to_all | solution.py:122
  749.5 46.9 %all-to-all-start = ((bf16[6,32,4,128]{3,2,0,1:T(4,128)(2,1)}), bf16[6,32,4,128]{3,2,0,1:T(4,128)(2,1)S(1)}, u32[]{:S(2)}, u32[]{:S(2)}) async-start(bf16[6,32,4,128]{3,2,0,1:T(4,128)(2,1)} %get-tuple-element.58), calls=%async_computation | async-start | bytes 393216 | tf_op jit(solution)/shard_map/all_to_all | solution.py:123
  787.1 23.0 %copy-start.21 = (bf16[24,8,8,128]{3,2,1,0:T(8,128)(2,1)}, bf16[24,8,8,128]{3,2,1,0:T(8,128)(2,1)S(1)}, u32[]{:S(2)}) copy-start(bf16[24,8,8,128]{3,2,1,0:T(8,128)(2,1)S(1)} %copy.471) | copy-start | bytes 1179652
  789.2 7.6 copy-start.48
  796.7 11.3 copy-start.37
  796.7 7.6 copy-start.39
  796.8 3.8 copy-start.41
  796.8 1.8 copy-start.43
  798.6 1.8 copy-start.18
  798.6 1.4 copy-start.29
  798.6 1.8 copy-start.51
  798.8 1.2 copy-start.10
  802.3 1.9 copy-start.16
  802.3 1.5 copy-start.26
  803.0 0.9 copy-start.8
  806.1 1.8 copy-start.14
  806.2 1.4 copy-start.23
  806.3 1.2 copy-start.6
  809.8 1.6 copy-start.12
  810.0 1.1 copy-start.4
  810.0 6.6 copy-start.59
  810.0 6.6 copy-start.61
  812.7 15.8 all-to-all-start.5
  816.6 1315.8 %reduce-scatter.4.cloned.1.call-start = ((), (), s32[]{:S(2)}) async-start(), calls=%async_computation.8 | async-start | bytes 8421376 | tf_op jit(solution)/shard_map/reduce_scatter | solution.py:140
  816.6 17.4 copy-start.55
  816.7 17.4 copy-start.57
  843.1 1.0 copy-start.30
  843.1 1.1 copy-start.27
  844.1 4.3 copy-start.24
  844.3 16.0 all-to-all-start.2
  849.5 12.7 copy-start.52
  860.3 1.1 copy-start.11
  860.3 1.9 copy-start.19
  860.3 1.9 copy-start.31
  861.2 12.7 copy-start.46
  862.2 1.4 copy-start.44
  862.7 0.9 copy-start.32
  864.1 4.8 copy-start.9
  867.1 2.6 copy-start.17
  867.1 2.6 copy-start.28
  867.1 2.6 copy-start.50
  869.8 1.3 copy-start.42
  871.6 2.3 copy-start.7
  872.0 2.6 copy-start.15
  872.1 2.6 copy-start.25
  874.7 1.3 copy-start.40
  876.0 1.3 copy-start.36
  876.9 2.2 copy-start.5
  876.9 2.2 copy-start.45
  877.3 2.5 copy-start.13
  877.3 2.5 copy-start.22
  879.9 1.0 copy-start.35
  880.9 5.8 copy-start.38
  882.5 5.2 copy-start.20
  882.5 16.5 all-to-all-start.4
  891.4 8.6 copy-start.56
  900.0 1233.8 %copy-start.1 = (bf16[1,128,1,4096]{3,1,2,0:T(8,128)(2,1)S(1)}, bf16[1,128,1,4096]{3,1,2,0:T(8,128)(2,1)}, u32[]{:S(2)}) copy-start(bf16[1,128,1,4096]{3,1,2,0:T(8,128)(2,1)} %param.15) | copy-start | bytes 3145732
  900.8 1231.6 %copy-start.47 = (bf16[16,512]{1,0:T(8,128)(2,1)S(1)}, bf16[16,512]{1,0:T(8,128)(2,1)}, u32[]{:S(2)}) copy-start(bf16[16,512]{1,0:T(8,128)(2,1)} %param.19) | copy-start | bytes 49156
  900.8 1231.6 %copy-start.53 = (f32[16,512]{1,0:T(8,128)S(1)}, f32[16,512]{1,0:T(8,128)}, u32[]{:S(2)}) copy-start(f32[16,512]{1,0:T(8,128)} %param.21) | copy-start | bytes 98308
  900.8 1231.6 %copy-start.54 = (f32[16,512]{1,0:T(8,128)S(1)}, f32[16,512]{1,0:T(8,128)}, u32[]{:S(2)}) copy-start(f32[16,512]{1,0:T(8,128)} %param.20) | copy-start | bytes 98308
  (5 other events, 3.6 us)
Sparse Core Ops, SparseCore 0:
  9.9 734.4 all-gather.1
  843.3 1289.0 reduce-scatter.3
where the time goes:
time: 2150 us; the launch traced here: 2140 us
  waiting for transfers between devices  1900 us (88%)
  local copies, waits for them, and re-layouts  65.1 us (3%)
  starting transfers between devices  52.6 us (2%)
  blocking collectives  50.5 us (2%)
  matrix products  33.8 us (2%)
    reduce_scatter x1, waiting for transfers between devices, body(): lax.psum_scatter(partial_sum, ('seq', 'fsdp'), scatter_dimension=0, tiled...  1230 us
    all_gather x1, waiting for transfers between devices, fetch_weight(): return lax.all_gather(value_weight, ('seq', 'fsdp'), axis=0, tiled=True)  641 us
    all_to_all x1, blocking collectives, body(): lax.all_to_all(query_send, 'seq', split_axis=1, concat_axis=1, tiled=True)  50.5 us
  transfers between devices with their start and end apart: 7, of which 6 were waited for; matrix products, arithmetic and copies ran while one was open for 4% of the time, Pallas kernels for 0%

commit v1 on v0

--- a/solution.py
+++ b/solution.py
@@ -81,7 +81,12 @@
 
 
 def fetch_weight(value_weight):
-    return lax.all_gather(value_weight, ("seq", "fsdp"), axis=0, tiled=True)
+    return jnp.concatenate(
+        lax.all_to_all(
+            jnp.stack([value_weight] * lax.axis_size(("seq", "fsdp"))), ("seq", "fsdp"), 0, 0
+        ),
+        axis=0,
+    )
 
 
 def body(inputs, queries, rotated_keys, out_grad, value_weight, fisher, anchor, doc_starts, owners):

time: 2150 us -> 1610 us (0.75)
  waiting for transfers between devices: 1900 us -> 1290 us
  blocking collectives: 50.5 us -> 157 us
  starting transfers between devices: 52.6 us -> 21.8 us
    all_gather x1 -> x0, waiting for transfers between devices: 641 us -> none  [fetch_weight(): return lax.all_gather(value_weight, ('seq', 'fsdp'), axis=0, tiled=True)]
    all_to_all x0 -> x1, blocking collectives: none -> 108 us  [fetch_weight(): lax.all_to_all(jnp.stack([value_weight] * lax.axis_size(('seq', 'fsdp')))...]
    all_to_all x1, starting transfers between devices: 34.9 us -> 4.95 us  [body(): lax.all_to_all(key_send, 'seq', split_axis=1, concat_axis=1, tiled=True)]
    all_to_all x1, waiting for transfers between devices: 0.01 us -> 23.4 us  [body(): lax.all_to_all(grad_send, 'seq', split_axis=1, concat_axis=1, tiled=True)]
  transfers between devices with their start and end apart: 7 -> 6, of which waited for: 6 -> 6; matrix products, arithmetic and copies ran while one was open for 4% -> 3% of each run, Pallas kernels for 0% -> 0%
where the time goes in v1:
time: 1610 us; the launch traced here: 1600 us
  waiting for transfers between devices  1290 us (80%)
  blocking collectives  157 us (10%)
  local copies, waits for them, and re-layouts  65.4 us (4%)
  matrix products  31.7 us (2%)
  starting transfers between devices  21.8 us (1%)
  other arithmetic  18.7 us (1%)
    reduce_scatter x1, waiting for transfers between devices, body(): lax.psum_scatter(partial_sum, ('seq', 'fsdp'), scatter_dimension=0, tiled...  1230 us
    all_to_all x1, blocking collectives, fetch_weight(): lax.all_to_all(jnp.stack([value_weight] * lax.axis_size(('seq', 'fsdp')))...  108 us
    all_to_all x1, blocking collectives, body(): lax.all_to_all(query_send, 'seq', split_axis=1, concat_axis=1, tiled=True)  49.4 us
  transfers between devices with their start and end apart: 6, of which 6 were waited for; matrix products, arithmetic and copies ran while one was open for 3% of the time, Pallas kernels for 0%

profile of v1, /device:TPU:0, one launch (start us, length us, event | category | flops | bytes accessed | tf_op | source)
XLA Modules:
  0.0 1599.4 jit_solution(2326362195158197606)
XLA Ops:
  9.9 5.6 gather_fusion.4
  15.5 2.7 gather_fusion.2
  18.2 3.9 broadcast_select_fusion
  22.1 2.9 reshape.293
  25.0 3.9 reshape.288
  28.9 3.6 copy_select_fusion
  32.5 49.4 %all_to_all.35 = bf16[6,32,4,1024]{3,2,0,1:T(4,128)(2,1)} all-to-all(bf16[6,32,4,1024]{3,2,0,1:T(4,128)(2,1)S(1)} %get-tuple-element.56), channel_id=1, replica_groups=mesh['seq'=32,'fsdp'=8] {'seq'}, dimensions={1} | all-to-all | bytes 3145728 | tf_op jit(solution)/shard_map/all_to_all | solution.py:126
  82.4 107.7 %all_to_all.36 = bf16[256,16,512]{2,1,0:T(8,128)(2,1)} all-to-all(bf16[256,16,512]{2,1,0:T(8,128)(2,1)S(1)} %stack.8), channel_id=1, replica_groups=mesh['seq'=32,'fsdp'=8] {'seq','fsdp'}, dimensions={0} | all-to-all | bytes 8388608 | tf_op jit(solution)/shard_map/all_to_all | solution.py:85
  190.1 4.6 all-to-all-start.4
  196.5 1.0 gather_fusion.1
  198.3 6.2 fusion.106
  204.8 0.8 copy.470
  205.8 0.8 copy.476
  206.9 0.8 copy.474
  207.9 0.8 copy.472
  208.8 0.8 convolution_convert_fusion.9
  209.5 1.0 gather_fusion.3
  210.8 1.0 copy_select_fusion.2
  211.8 23.4 %all-to-all-done.4 = bf16[6,32,4,1024]{3,2,0,1:T(4,128)(2,1)S(1)} async-done(((bf16[6,32,4,1024]{3,2,0,1:T(4,128)(2,1)}), bf16[6,32,4,1024]{3,2,0,1:T(4,128)(2,1)S(1)}, u32[]{:S(2)}, u32[]{:S(2)}) %all-to-all-start.4) | async-done | bytes 1572896 | tf_op jit(solution)/shard_map/all_to_all | solution.py:127
  235.2 5.0 all-to-all-start
  240.2 2.3 fusion.105
  243.0 0.8 copy.477
  244.1 0.8 copy.475
  245.2 0.8 copy.473
  246.0 6.5 all-to-all-done
  252.9 1.8 fusion.115
  254.9 1.2 copy-done.11
  256.7 1.8 fusion.112
  259.1 0.9 copy-done.9
  260.5 1.8 fusion.109
  262.5 1.2 copy-done.7
  264.2 1.8 fusion.118
  266.2 1.0 copy-done.5
  267.7 1.1 pad_maximum_fusion.2
  268.8 3.9 all-to-all-start.6
  272.8 11.8 all-to-all-done.6
  284.7 0.8 gather_fusion.6
  285.6 4.6 convolution_bitcast_fusion
  290.1 9.1 copy.468
  299.2 1.0 copy-done.31
  300.4 4.1 all-to-all-start.3
  304.6 1.1 bitcast_convert_fusion.3
  305.6 10.5 all-to-all-done.3
  317.3 0.8 fusion.29
  318.5 0.9 copy-done.33
  319.9 1.1 copy.397
  321.0 1.9 stack_reshape.37
  322.9 1.7 fusion.42
  324.8 0.8 fusion.34
  326.0 0.9 copy-done.34
  327.9 1.7 fusion.43
  329.7 0.8 fusion.39
  330.5 1.2 fusion.11
  333.1 1.6 fusion.44
  334.9 0.8 fusion.24
  337.1 1.1 pad_maximum_fusion.1
  338.3 4.2 all-to-all-start.5
  343.7 1.2 copy.416
  344.9 2.4 reshape.294
  347.3 8.1 all-to-all-done.5
  355.5 1.0 gather_fusion.5
  357.2 4.7 fusion.4
  361.9 1229.0 %reduce-scatter.4.cloned.1.call-done = f32[16,512]{1,0:T(8,128)} async-done(((f32[4096,512]{1,0:T(8,128)}), f32[16,512]{1,0:T(8,128)}) %reduce-scatter.4.cloned.1.call-update) | async-done | bytes 32784 | tf_op jit(solution)/shard_map/reduce_scatter | solution.py:145
  1590.9 1.4 multiply_add_fusion
  (218 shorter events, 19.9 us)
Async XLA Ops:
  7.2 201.6 %copy-start = (bf16[1,128,1,4096]{3,1,2,0:T(8,128)(2,1)S(1)}, bf16[1,128,1,4096]{3,1,2,0:T(8,128)(2,1)}, u32[]{:S(2)}) copy-start(bf16[1,128,1,4096]{3,1,2,0:T(8,128)(2,1)} %param.15) | copy-start | bytes 3145732
  9.9 5.6 copy-start.2
  32.5 49.4 %copy-start.48 = (bf16[16,512]{1,0:T(8,128)(2,1)S(1)}, bf16[16,512]{1,0:T(8,128)(2,1)}, u32[]{:S(2)}) copy-start(bf16[16,512]{1,0:T(8,128)(2,1)} %param.19) | copy-start | bytes 49156
  190.1 6.5 copy-start.4
  190.1 45.1 %all-to-all-start.4 = ((bf16[6,32,4,1024]{3,2,0,1:T(4,128)(2,1)}), bf16[6,32,4,1024]{3,2,0,1:T(4,128)(2,1)S(1)}, u32[]{:S(2)}, u32[]{:S(2)}) async-start(bf16[6,32,4,1024]{3,2,0,1:T(4,128)(2,1)} %get-tuple-element.55), calls=%async_computation.4 | async-start | bytes 3145728 | tf_op jit(solution)/shard_map/all_to_all | solution.py:127
  205.8 2.9 copy-start.3
  235.2 17.3 %all-to-all-start = ((bf16[6,32,4,128]{3,2,0,1:T(4,128)(2,1)}), bf16[6,32,4,128]{3,2,0,1:T(4,128)(2,1)S(1)}, u32[]{:S(2)}, u32[]{:S(2)}) async-start(bf16[6,32,4,128]{3,2,0,1:T(4,128)(2,1)} %get-tuple-element.58), calls=%async_computation | async-start | bytes 393216 | tf_op jit(solution)/shard_map/all_to_all | solution.py:128
  242.8 23.4 %copy-start.22 = (bf16[24,8,8,128]{3,2,1,0:T(8,128)(2,1)}, bf16[24,8,8,128]{3,2,1,0:T(8,128)(2,1)S(1)}, u32[]{:S(2)}) copy-start(bf16[24,8,8,128]{3,2,1,0:T(8,128)(2,1)S(1)} %copy.471) | copy-start | bytes 1179652
  244.9 8.0 copy-start.50
  252.8 11.3 copy-start.38
  252.8 7.6 copy-start.40
  252.9 3.8 copy-start.42
  252.9 1.8 copy-start.44
  254.7 1.8 copy-start.19
  254.7 1.4 copy-start.30
  254.8 1.8 copy-start.53
  254.9 1.2 copy-start.11
  258.5 1.9 copy-start.17
  258.5 1.5 copy-start.27
  262.3 1.8 copy-start.15
  262.3 1.4 copy-start.24
  262.5 1.2 copy-start.7
  265.9 1.6 copy-start.13
  266.1 1.0 copy-start.5
  266.1 6.6 copy-start.61
  266.2 6.6 copy-start.63
  268.8 15.8 all-to-all-start.6
  272.7 1318.2 %reduce-scatter.4.cloned.1.call-start = ((), (), s32[]{:S(2)}) async-start(), calls=%async_computation.8 | async-start | bytes 8421376 | tf_op jit(solution)/shard_map/reduce_scatter | solution.py:145
  272.8 17.4 %copy-start.57 = (pred[128]{0:T(512)(128)(4,1)}, pred[128]{0:T(512)(128)(4,1)S(1)}, u32[]{:S(2)}) copy-start(pred[128]{0:T(512)(128)(4,1)S(1)} %get-tuple-element.37) | copy-start | bytes 388
  272.8 17.4 %copy-start.59 = (s32[1024]{0:T(1024)}, s32[1024]{0:T(1024)S(1)}, u32[]{:S(2)}) copy-start(s32[1024]{0:T(1024)S(1)} %pad_clamp_fusion) | copy-start | bytes 12292
  299.2 1.0 copy-start.31
  299.2 1.1 copy-start.28
  300.2 4.3 copy-start.25
  300.4 15.7 all-to-all-start.3
  305.6 12.4 copy-start.54
  316.1 1.1 copy-start.12
  316.1 1.9 copy-start.20
  316.1 1.9 copy-start.32
  317.0 12.7 copy-start.47
  318.1 1.4 copy-start.45
  318.5 0.9 copy-start.33
  319.9 4.8 copy-start.10
  322.9 2.6 copy-start.18
  322.9 2.6 copy-start.29
  322.9 2.6 copy-start.52
  325.6 1.3 copy-start.43
  327.4 2.3 copy-start.8
  327.9 2.6 copy-start.16
  327.9 2.6 copy-start.26
  330.5 1.3 copy-start.41
  331.8 1.3 copy-start.37
  332.7 2.2 copy-start.6
  332.7 2.2 copy-start.46
  333.1 2.5 copy-start.14
  333.1 2.5 copy-start.23
  335.7 1.0 copy-start.36
  336.7 5.9 copy-start.39
  338.3 5.2 copy-start.21
  338.3 17.1 %all-to-all-start.5 = ((bf16[6,32,4,128]{3,2,0,1:T(4,128)(2,1)}), bf16[6,32,4,128]{3,2,0,1:T(4,128)(2,1)S(1)}, u32[]{:S(2)}, u32[]{:S(2)}) async-start(bf16[6,32,4,128]{3,2,0,1:T(4,128)(2,1)} %pad_maximum_fusion.1), calls=%async_computation.5 | async-start | bytes 393216 | tf_op jit(solution)/shard_map/all_to_all | solution.py:133
  347.3 9.2 copy-start.58
  356.5 1235.8 %copy-start.1 = (bf16[1,128,1,4096]{3,1,2,0:T(8,128)(2,1)S(1)}, bf16[1,128,1,4096]{3,1,2,0:T(8,128)(2,1)}, u32[]{:S(2)}) copy-start(bf16[1,128,1,4096]{3,1,2,0:T(8,128)(2,1)} %param.15) | copy-start | bytes 3145732
  357.2 1233.6 %copy-start.49 = (bf16[16,512]{1,0:T(8,128)(2,1)S(1)}, bf16[16,512]{1,0:T(8,128)(2,1)}, u32[]{:S(2)}) copy-start(bf16[16,512]{1,0:T(8,128)(2,1)} %param.19) | copy-start | bytes 49156
  357.2 1233.6 %copy-start.55 = (f32[16,512]{1,0:T(8,128)S(1)}, f32[16,512]{1,0:T(8,128)}, u32[]{:S(2)}) copy-start(f32[16,512]{1,0:T(8,128)} %param.21) | copy-start | bytes 98308
  357.2 1233.6 %copy-start.56 = (f32[16,512]{1,0:T(8,128)S(1)}, f32[16,512]{1,0:T(8,128)}, u32[]{:S(2)}) copy-start(f32[16,512]{1,0:T(8,128)} %param.20) | copy-start | bytes 98308
  (6 other events, 4.3 us)
Sparse Core Ops, SparseCore 0:
  299.3 1291.4 reduce-scatter.3
